TPU v7x, 32 devices: a whole 2x2x4 slice. The times are simulated.
32 devices in a mesh: chan: 8 (over z, core), tm: 4 (over y, x).
Axes of the slice: x: 2, y: 2, z: 4, core: 2. Of those that a mesh axis runs over, the one named last changes fastest.
Arguments:
- spectra: bfloat16 [4, 1024, 1024], P('tm', 'chan')
- tile_bin: int32 [32], P('chan'), may hold values from 0 to 7
- owner_bins: int32 [8], replicated, may hold values from 0 to 7, each once
- source_slab: int32 [1], replicated, may hold values from 0 to 255
Outputs:
- stacks: float32 [8, 128, 512], P('chan', 'tm')
Inputs may be any that keep to these rules, and one draw needn't show every extreme that they name: `tile_bin`: a tile of 128 pairs belongs to exactly one offset bin. `owner_bins`: every bin stands once. `source_slab`: the slab's 4 channels lie within one chan index's block.
All inputs are finite; a program needn't handle non-finite values.
Results may differ from a plain program's by a relative error of at most 0.005.
Values may be sent and summed in bfloat16 or wider, within the bound.
A program may use at most 64 MiB of HBM per device.

v0:
```python
import math

import jax
import jax.numpy as jnp
from jax import lax
from jax.sharding import PartitionSpec as P

LAGS = 512
SEG_LEN = 15000
K0 = 60
GROUP = 64
SRC = 4
PAIRS = 128


def shifted(block, axis, distance):
    devices = range(lax.axis_size(axis))
    route = [((i - distance) % len(devices), i) for i in devices]
    return lax.ppermute(block, axis, route)


def whiten_block(raw_block):
    values = raw_block.astype(jnp.float32)
    channels = values.shape[0]
    bands = values.shape[1] // 2
    grouped = values.reshape(channels, 2, bands // GROUP, GROUP)
    power = jnp.mean(grouped[:, 0] * grouped[:, 0] + grouped[:, 1] * grouped[:, 1], axis=-1)
    inverse = 1.0 / jnp.sqrt(power + 1e-06)
    return (grouped * inverse[:, None, :, None]).reshape(channels, 2 * bands).astype(jnp.bfloat16)


def phase_tables(bands, lag_count):
    freq_index = K0 + jnp.arange(bands)
    lag_index = jnp.arange(lag_count) - lag_count // 2
    phase = freq_index[:, None] * lag_index[None, :] % SEG_LEN
    angle = phase.astype(jnp.float32) * (2.0 * math.pi / SEG_LEN)
    return (jnp.cos(angle), jnp.sin(angle))


def modulate(slab_rows, cosines, sines):
    values = slab_rows.astype(jnp.float32)
    bands = cosines.shape[0]
    real_part = values[:, :bands, None]
    imag_part = values[:, bands:, None]
    upper = real_part * cosines[None] + imag_part * sines[None]
    lower = imag_part * cosines[None] - real_part * sines[None]
    return jnp.concatenate([upper, lower], axis=1).astype(jnp.bfloat16)


def normalize(correlation):
    energy = jnp.mean(correlation * correlation, axis=-1, keepdims=True)
    return correlation / jnp.sqrt(energy + 1e-06)


def per_device(spectra, tile_bin, owner_bins, source_slab):
    whitened = whiten_block(spectra[0])
    channels = whitened.shape[0]
    bands = whitened.shape[1] // 2
    cycle_size = lax.axis_size("chan")
    my_index = lax.axis_index("chan")
    slabs_per_block = channels // SRC
    slab_number = source_slab[0]
    root_index = slab_number // slabs_per_block
    own_slab = lax.dynamic_slice_in_dim(whitened, slab_number % slabs_per_block * SRC, SRC, 0)
    initial = jnp.where(my_index == root_index, own_slab, jnp.zeros_like(own_slab))

    def paired_hop(hop_count, state):
        ahead, behind, received = state
        ahead = shifted(ahead, "chan", 1)
        behind = shifted(behind, "chan", -1)
        received = jnp.where((my_index - hop_count) % cycle_size == root_index, ahead, received)
        received = jnp.where((my_index + hop_count) % cycle_size == root_index, behind, received)
        return (ahead, behind, received)

    source_rows = lax.fori_loop(1, cycle_size // 2 + 1, paired_hop, (own_slab, own_slab, initial))[
        2
    ]
    cosines, sines = phase_tables(bands, LAGS)
    modulated = modulate(source_rows, cosines, sines)
    correlation = jnp.einsum("ck,ikl->icl", whitened, modulated, preferred_element_type=jnp.float32)
    traces = normalize(correlation)
    summed = lax.psum(traces, "tm")
    row_count = PAIRS // lax.axis_size("tm")
    own_rows = lax.dynamic_slice_in_dim(summed, lax.axis_index("tm") * row_count, row_count, 1)
    membership = (owner_bins[:, None] == tile_bin[None, :]).astype(jnp.float32)
    stacked = lax.psum_scatter(
        jnp.einsum("rt,tpl->rpl", membership, own_rows, precision=lax.Precision.HIGHEST),
        "chan",
        scatter_dimension=0,
        tiled=True,
    )
    return stacked / lax.axis_size("tm")


def solution(mesh):
    return jax.shard_map(
        per_device,
        mesh=mesh,
        in_specs=(P("tm", "chan", None), P("chan"), P(), P()),
        out_specs=P("chan", "tm", None),
        check_vma=False,
    )
```

profile of v0, /device:TPU:0, one launch (start us, length us, event | category | flops | bytes accessed | tf_op | source)
XLA Modules:
  0.0 135.3 jit_solution(4743199806616281129)
XLA Ops:
  7.3 1.1 copy.14
  9.0 24.5 %while.19 = (s32[]{:T(128)}, bf16[4,1024]{1,0:T(4,128)(2,1)S(1)}, bf16[4,1024]{1,0:T(4,128)(2,1)S(1)}, bf16[4,1024]{1,0:T(4,128)(2,1)S(1)}, s32[]{:T(128)}, /*in...) while((s32[]{:T(128)}, bf16[4,1024]{1,0:T(4,128)(2,1)S(1)}, bf16[4,1024]{1,0:T(4,128)(2,1)S(1)}, ...), condition=%wide.region_2.3_spmd, body=%wide.region_1.2_spmd.sunk | while | flops 8220 | bytes 131515 | solution.py:75
  9.0 4.5 %collective-permute-start.1 = (bf16[4,1024]{1,0:T(4,128)(2,1)S(1)}, bf16[4,1024]{1,0:T(4,128)(2,1)S(1)}, u32[]{:S(2)}, u32[]{:S(2)}) collective-permute-start(bf16[4,1024]{1,0:T(4,128)(2,1)S(1)} %get-tuple-element.246), channel_id=1, source_target_pairs={{4,0},{8,4},{12,8},{16,12},{20,16},{24,20},{28,24},{0,28},{5,1},{9... | collective-permute-start | bytes 24584 | tf_op jit(solution)/shard_map/while/body/eval_jaxpr/ppermute | solution.py:19
  13.6 1.4 %collective-permute-done.1 = bf16[4,1024]{1,0:T(4,128)(2,1)S(1)} collective-permute-done((bf16[4,1024]{1,0:T(4,128)(2,1)S(1)}, bf16[4,1024]{1,0:T(4,128)(2,1)S(1)}, u32[]{:S(2)}, u32[]{:S(2)}) %collective-permute-start.1) | collective-permute-done | bytes 8224 | tf_op jit(solution)/shard_map/while/body/eval_jaxpr/ppermute | solution.py:19
  15.0 3.5 %collective-permute-done = bf16[4,1024]{1,0:T(4,128)(2,1)S(1)} collective-permute-done((bf16[4,1024]{1,0:T(4,128)(2,1)S(1)}, bf16[4,1024]{1,0:T(4,128)(2,1)S(1)}, u32[]{:S(2)}, u32[]{:S(2)}) %collective-permute-start) | collective-permute-done | bytes 8224 | tf_op jit(solution)/shard_map/while/body/eval_jaxpr/ppermute | solution.py:19
  18.6 0.5 collective-permute-start
  19.1 0.9 collective-permute-done.1
  19.9 3.5 %collective-permute-done = bf16[4,1024]{1,0:T(4,128)(2,1)S(1)} collective-permute-done((bf16[4,1024]{1,0:T(4,128)(2,1)S(1)}, bf16[4,1024]{1,0:T(4,128)(2,1)S(1)}, u32[]{:S(2)}, u32[]{:S(2)}) %collective-permute-start) | collective-permute-done | bytes 8224 | tf_op jit(solution)/shard_map/while/body/eval_jaxpr/ppermute | solution.py:19
  23.6 0.4 collective-permute-start
  24.1 0.9 collective-permute-done.1
  25.0 3.5 %collective-permute-done = bf16[4,1024]{1,0:T(4,128)(2,1)S(1)} collective-permute-done((bf16[4,1024]{1,0:T(4,128)(2,1)S(1)}, bf16[4,1024]{1,0:T(4,128)(2,1)S(1)}, u32[]{:S(2)}, u32[]{:S(2)}) %collective-permute-start) | collective-permute-done | bytes 8224 | tf_op jit(solution)/shard_map/while/body/eval_jaxpr/ppermute | solution.py:19
  28.6 0.5 collective-permute-start
  29.1 0.9 collective-permute-done.1
  30.0 3.5 %collective-permute-done = bf16[4,1024]{1,0:T(4,128)(2,1)S(1)} collective-permute-done((bf16[4,1024]{1,0:T(4,128)(2,1)S(1)}, bf16[4,1024]{1,0:T(4,128)(2,1)S(1)}, u32[]{:S(2)}, u32[]{:S(2)}) %collective-permute-start) | collective-permute-done | bytes 8224 | tf_op jit(solution)/shard_map/while/body/eval_jaxpr/ppermute | solution.py:19
  33.6 4.3 %fusion.9 = (f32[512,512]{0,1:T(8,128)S(1)}, f32[512,512]{0,1:T(8,128)S(1)}) fusion(s32[512]{0:T(512)S(1)} %get-tuple-element.195, s32[512]{0:T(512)S(1)} %get-tuple-element.196), kind=kLoop, calls=%fused_computation.16 | loop fusion | flops 2359296 | bytes 2101248 | tf_op jit(solution)/shard_map/cos | solution.py:37
  37.9 1.1 add_convert_fusion
  39.0 1.3 multiply_reduce_fusion
  40.3 1.1 divide_bitcast_fusion
  41.5 50.9 %all-reduce.2.cloned.1.call-done = f32[4,128,512]{1,2,0:T(8,128)} async-done(((f32[4,128,512]{1,2,0:T(8,128)}), f32[4,128,512]{1,2,0:T(8,128)}) %all-reduce.2.cloned.1.call-update) | async-done | bytes 1048592 | tf_op jit(solution)/shard_map/psum | solution.py:82
  92.3 1.6 %constant_dynamic-slice_fusion = f32[4,32,512]{1,2,0:T(8,128)S(1)} fusion(f32[4,128,512]{1,2,0:T(8,128)} %all-reduce.2.cloned.1.call-done, s32[]{:T(128)S(6)} %select_n.118), kind=kLoop, calls=%fused_computation.36 | loop fusion | bytes 524292 | tf_op jit(solution)/shard_map/dynamic_slice | solution.py:84
  94.3 0.5 fusion.15
  94.8 1.1 copy.20
  95.9 31.1 %reduce-scatter.2.cloned.1.call-done = f32[1,32,512]{2,1,0:T(8,128)} async-done(((f32[8,32,512]{2,1,0:T(8,128)}), f32[1,32,512]{2,1,0:T(8,128)}) %reduce-scatter.2.cloned.1.call-update) | async-done | bytes 65552 | tf_op jit(solution)/shard_map/reduce_scatter | solution.py:86
  127.0 1.5 %broadcast_multiply_fusion = f32[1,32,512]{2,1,0:T(8,128)} fusion(f32[1,32,512]{2,1,0:T(8,128)} %reduce-scatter.2.cloned.1.call-done), kind=kLoop, calls=%fused_computation.26 | loop fusion | flops 16384 | bytes 131072 | tf_op jit(solution)/shard_map/div | solution.py:92
  (36 shorter events, 1.4 us)
Async XLA Ops:
  6.5 85.8 %all-reduce.2.cloned.1.call-start = ((), (), s32[]{:S(2)}) async-start(), calls=%async_computation.1 | async-start | bytes 2097152 | tf_op jit(solution)/shard_map/psum | solution.py:82
  9.0 5.9 %collective-permute-start.1 = (bf16[4,1024]{1,0:T(4,128)(2,1)S(1)}, bf16[4,1024]{1,0:T(4,128)(2,1)S(1)}, u32[]{:S(2)}, u32[]{:S(2)}) collective-permute-start(bf16[4,1024]{1,0:T(4,128)(2,1)S(1)} %get-tuple-element.246), channel_id=1, source_target_pairs={{4,0},{8,4},{12,8},{16,12},{20,16},{24,20},{28,24},{0,28},{5,1},{9... | collective-permute-start | bytes 24584 | tf_op jit(solution)/shard_map/while/body/eval_jaxpr/ppermute | solution.py:19
  13.6 4.9 %collective-permute-start = (bf16[4,1024]{1,0:T(4,128)(2,1)S(1)}, bf16[4,1024]{1,0:T(4,128)(2,1)S(1)}, u32[]{:S(2)}, u32[]{:S(2)}) collective-permute-start(bf16[4,1024]{1,0:T(4,128)(2,1)S(1)} %get-tuple-element.245), channel_id=1, source_target_pairs={{28,0},{0,4},{4,8},{8,12},{12,16},{16,20},{20,24},{24,28},{29,1},{... | collective-permute-start | bytes 24584 | tf_op jit(solution)/shard_map/while/body/eval_jaxpr/ppermute | solution.py:19
  18.5 1.4 %collective-permute-start.1 = (bf16[4,1024]{1,0:T(4,128)(2,1)S(1)}, bf16[4,1024]{1,0:T(4,128)(2,1)S(1)}, u32[]{:S(2)}, u32[]{:S(2)}) collective-permute-start(bf16[4,1024]{1,0:T(4,128)(2,1)S(1)} %get-tuple-element.246), channel_id=1, source_target_pairs={{4,0},{8,4},{12,8},{16,12},{20,16},{24,20},{28,24},{0,28},{5,1},{9... | collective-permute-start | bytes 24584 | tf_op jit(solution)/shard_map/while/body/eval_jaxpr/ppermute | solution.py:19
  18.6 4.9 %collective-permute-start = (bf16[4,1024]{1,0:T(4,128)(2,1)S(1)}, bf16[4,1024]{1,0:T(4,128)(2,1)S(1)}, u32[]{:S(2)}, u32[]{:S(2)}) collective-permute-start(bf16[4,1024]{1,0:T(4,128)(2,1)S(1)} %get-tuple-element.245), channel_id=1, source_target_pairs={{28,0},{0,4},{4,8},{8,12},{12,16},{16,20},{20,24},{24,28},{29,1},{... | collective-permute-start | bytes 24584 | tf_op jit(solution)/shard_map/while/body/eval_jaxpr/ppermute | solution.py:19
  23.5 1.5 %collective-permute-start.1 = (bf16[4,1024]{1,0:T(4,128)(2,1)S(1)}, bf16[4,1024]{1,0:T(4,128)(2,1)S(1)}, u32[]{:S(2)}, u32[]{:S(2)}) collective-permute-start(bf16[4,1024]{1,0:T(4,128)(2,1)S(1)} %get-tuple-element.246), channel_id=1, source_target_pairs={{4,0},{8,4},{12,8},{16,12},{20,16},{24,20},{28,24},{0,28},{5,1},{9... | collective-permute-start | bytes 24584 | tf_op jit(solution)/shard_map/while/body/eval_jaxpr/ppermute | solution.py:19
  23.6 4.9 %collective-permute-start = (bf16[4,1024]{1,0:T(4,128)(2,1)S(1)}, bf16[4,1024]{1,0:T(4,128)(2,1)S(1)}, u32[]{:S(2)}, u32[]{:S(2)}) collective-permute-start(bf16[4,1024]{1,0:T(4,128)(2,1)S(1)} %get-tuple-element.245), channel_id=1, source_target_pairs={{28,0},{0,4},{4,8},{8,12},{12,16},{16,20},{20,24},{24,28},{29,1},{... | collective-permute-start | bytes 24584 | tf_op jit(solution)/shard_map/while/body/eval_jaxpr/ppermute | solution.py:19
  28.5 1.4 %collective-permute-start.1 = (bf16[4,1024]{1,0:T(4,128)(2,1)S(1)}, bf16[4,1024]{1,0:T(4,128)(2,1)S(1)}, u32[]{:S(2)}, u32[]{:S(2)}) collective-permute-start(bf16[4,1024]{1,0:T(4,128)(2,1)S(1)} %get-tuple-element.246), channel_id=1, source_target_pairs={{4,0},{8,4},{12,8},{16,12},{20,16},{24,20},{28,24},{0,28},{5,1},{9... | collective-permute-start | bytes 24584 | tf_op jit(solution)/shard_map/while/body/eval_jaxpr/ppermute | solution.py:19
  28.6 4.9 %collective-permute-start = (bf16[4,1024]{1,0:T(4,128)(2,1)S(1)}, bf16[4,1024]{1,0:T(4,128)(2,1)S(1)}, u32[]{:S(2)}, u32[]{:S(2)}) collective-permute-start(bf16[4,1024]{1,0:T(4,128)(2,1)S(1)} %get-tuple-element.245), channel_id=1, source_target_pairs={{28,0},{0,4},{4,8},{8,12},{12,16},{16,20},{20,24},{24,28},{29,1},{... | collective-permute-start | bytes 24584 | tf_op jit(solution)/shard_map/while/body/eval_jaxpr/ppermute | solution.py:19
  41.4 52.8 %copy-start = (s32[8]{0:T(128)S(1)}, s32[8]{0:T(128)}, u32[]{:S(2)}) copy-start(s32[8]{0:T(128)} %param.8) | copy-start | bytes 100
  41.4 52.8 %copy-start.1 = (s32[4]{0:T(128)S(1)}, s32[4]{0:T(128)}, u32[]{:S(2)}) copy-start(s32[4]{0:T(128)} %param.7) | copy-start | bytes 52
  41.4 85.5 %reduce-scatter.2.cloned.1.call-start = ((), (), s32[]{:S(2)}) async-start(), calls=%async_computation.2 | async-start | bytes 589824 | tf_op jit(solution)/shard_map/reduce_scatter | solution.py:86
Sparse Core Ops, SparseCore 0:
  41.6 50.7 all-reduce.1
  96.0 30.9 reduce-scatter.1
where the time goes:
time: 136 us; the launch traced here: 135 us
  waiting for transfers between devices  100 us (74%)
  between operations  14.2 us (10%)
  other arithmetic  8.38 us (6%)
  starting transfers between devices  6.27 us (5%)
  local copies, waits for them, and re-layouts  4.45 us (3%)
  matrix products  1.77 us (1%)
    psum x1, waiting for transfers between devices, per_device(): summed = lax.psum(traces, 'tm')  50.9 us
    reduce_scatter x1, waiting for transfers between devices, per_device(): lax.psum_scatter(jnp.einsum('rt,tpl->rpl', membership, own_rows, precisio...  31.1 us
    ppermute x8, waiting for transfers between devices, shifted(): return lax.ppermute(block, axis, route)  18.1 us
    ppermute x8, starting transfers between devices, shifted(): return lax.ppermute(block, axis, route)  6.23 us
    cos x1, other arithmetic, phase_tables(): return (jnp.cos(angle), jnp.sin(angle))  4.29 us
  transfers between devices with their start and end apart: 10, of which 10 were waited for; matrix products, arithmetic and copies ran while one was open for 0% of the time, Pallas kernels for 0%

commit v1 on v0

v1 whole, which is shorter than its diff:
```python
import functools
import math

import jax
import jax.numpy as jnp
import numpy as np
from jax import lax
from jax.experimental import pallas as pl
from jax.experimental.pallas import tpu as pltpu
from jax.sharding import PartitionSpec as P

LAGS = 512
SEG_LEN = 15000
K0 = 60
GROUP = 64
SRC = 4
PAIRS = 128
WIDE = 256
CHUNKS = 2
MESH = pl.DeviceIdType.MESH


def phase_table(bands):
    phase = (K0 + np.arange(bands))[:, None] * (np.arange(LAGS) - LAGS // 2)[None, :] % SEG_LEN
    angle = phase.astype(np.float64) * (2.0 * math.pi / SEG_LEN)
    return jnp.asarray(np.concatenate([np.cos(angle), np.sin(angle)]), dtype=jnp.bfloat16)


def whiten(real_part, imag_part, same_group):
    power = (real_part * real_part + imag_part * imag_part) * (1.0 / GROUP)
    high = power.astype(jnp.bfloat16)
    low = (power - high.astype(jnp.float32)).astype(jnp.bfloat16)
    mean = jnp.dot(high, same_group, preferred_element_type=jnp.float32)
    mean = mean + jnp.dot(low, same_group, preferred_element_type=jnp.float32)
    inverse = lax.rsqrt(mean + 1e-06)
    return [
        (part * inverse).astype(jnp.bfloat16).astype(jnp.float32)
        for part in (real_part, imag_part)
    ]


def kernel(
    n_chan, n_tm, tile_bin, owner_bins, source_slab, spectra, table_in, out,
    block, table, white, slabs, own, t_out, t_in, c_out, c_in,
    local_sems, s_send, s_recv, t_send, t_recv, c_send, c_recv,
):
    channels, columns = block.shape
    bands = columns // 2
    halves = bands // WIDE
    rows = channels // n_tm
    width = LAGS // CHUNKS
    chan = lax.axis_index("chan")
    tm = lax.axis_index("tm")
    near = 1
    while near * near * 4 <= n_tm:
        near *= 2
    near = n_tm // near
    tm_peer = []
    for off in range(n_tm):
        far_step, near_step = off // near, off % near
        far_at = lax.rem(tm // near + far_step, n_tm // near)
        tm_peer.append(far_at * near + lax.rem(lax.rem(tm, near) + near_step, near))
    chan_peer = [lax.rem(chan + off, n_chan) for off in range(n_chan)]

    barrier = pltpu.get_barrier_semaphore()
    for off in range(1, n_chan):
        pl.semaphore_signal(barrier, inc=1, device_id=(chan_peer[off], tm), device_id_type=MESH)
    for off in range(1, n_tm):
        pl.semaphore_signal(barrier, inc=1, device_id=(chan, tm_peer[off]), device_id_type=MESH)
    load_block = pltpu.make_async_copy(spectra.at[0], block, local_sems.at[0])
    load_table = pltpu.make_async_copy(table_in, table, local_sems.at[1])
    load_block.start()
    load_table.start()

    slab = source_slab[0]
    slabs_per_block = channels // SRC
    root = slab // slabs_per_block
    first_row = lax.rem(slab, slabs_per_block) * SRC
    blocks = columns // WIDE
    pick_row = lax.broadcasted_iota(jnp.int32, (SRC * blocks, channels), 0)
    pick_col = lax.broadcasted_iota(jnp.int32, (SRC * blocks, channels), 1)
    same_group = (
        lax.broadcasted_iota(jnp.int32, (WIDE, WIDE), 0) // GROUP
        == lax.broadcasted_iota(jnp.int32, (WIDE, WIDE), 1) // GROUP
    )
    same_group = jnp.where(same_group, 1.0, 0.0).astype(jnp.bfloat16)

    load_block.wait()
    picked = jnp.zeros((SRC * blocks, WIDE), jnp.float32)
    for c in range(blocks):
        chosen = pick_row - SRC * c == pick_col - first_row
        chosen = chosen & (pick_row >= SRC * c) & (pick_row < SRC * (c + 1))
        picked = picked + jnp.dot(
            jnp.where(chosen, 1.0, 0.0).astype(jnp.bfloat16),
            block[:, c * WIDE : (c + 1) * WIDE],
            preferred_element_type=jnp.float32,
        )
    slabs[0] = picked.astype(jnp.bfloat16)
    pl.semaphore_wait(barrier, n_chan + n_tm - 2)
    slab_copies = []
    for off in range(1, n_chan):
        copy = pltpu.make_async_remote_copy(
            src_ref=slabs.at[0],
            dst_ref=slabs.at[off],
            send_sem=s_send.at[off - 1],
            recv_sem=s_recv.at[off - 1],
            device_id=(chan_peer[off], tm),
            device_id_type=MESH,
        )
        copy.start()
        slab_copies.append(copy)

    for h in range(halves):
        real_at = slice(h * WIDE, (h + 1) * WIDE)
        imag_at = slice(bands + h * WIDE, bands + (h + 1) * WIDE)
        white[:, real_at], white[:, imag_at] = whiten(
            block[:, real_at].astype(jnp.float32),
            block[:, imag_at].astype(jnp.float32),
            same_group,
        )
    for copy in slab_copies:
        copy.wait_recv()
    source = slabs[lax.rem(chan - root + n_chan, n_chan)].astype(jnp.float32)
    source_real, source_imag = whiten(
        source[: SRC * halves], source[SRC * halves :], same_group
    )
    load_table.wait()

    t_copies = [[] for _ in range(CHUNKS)]
    for off in [*reversed(range(1, n_tm)), 0]:
        at = pl.ds(pl.multiple_of(tm_peer[off] * rows, rows), rows)
        products = []
        for i in range(SRC):
            upper, lower = [], []
            for h in range(halves):
                a = white[at, h * WIDE : (h + 1) * WIDE]
                b = white[at, bands + h * WIDE : bands + (h + 1) * WIDE]
                c = source_real[h * SRC + i : h * SRC + i + 1]
                d = source_imag[h * SRC + i : h * SRC + i + 1]
                upper.append(a * c + b * d)
                lower.append(a * d - b * c)
            products.append(jnp.concatenate(upper + lower, axis=1))
        product = jnp.concatenate(products, axis=0).astype(jnp.bfloat16)
        correlation = jnp.dot(product, table[...], preferred_element_type=jnp.float32)
        energy = jnp.mean(correlation * correlation, axis=-1, keepdims=True)
        traces = correlation * (lax.rsqrt(energy + 1e-06) * (1.0 / n_tm))
        if off == 0:
            own[...] = traces
            continue
        for h in range(CHUNKS):
            t_out[off - 1, h] = traces[:, h * width : (h + 1) * width].astype(jnp.bfloat16)
            copy = pltpu.make_async_remote_copy(
                src_ref=t_out.at[off - 1, h],
                dst_ref=t_in.at[off - 1, h],
                send_sem=t_send.at[off - 1, h],
                recv_sem=t_recv.at[off - 1, h],
                device_id=(chan, tm_peer[off]),
                device_id_type=MESH,
            )
            copy.start()
            t_copies[h].append(copy)

    c_copies = [[] for _ in range(CHUNKS)]
    for h in range(CHUNKS):
        summed = own[:, h * width : (h + 1) * width]
        for n, copy in enumerate(t_copies[h]):
            copy.wait_recv()
            summed = summed + t_in[n_tm - 2 - n, h].astype(jnp.float32)
        for off in [*range(1, n_chan), 0]:
            bin_here = owner_bins[chan_peer[off]]
            binned = jnp.zeros((rows, width), jnp.float32)
            for i in range(SRC):
                member = jnp.where(tile_bin[i] == bin_here, 1.0, 0.0)
                binned = binned + summed[i * rows : (i + 1) * rows] * member
            if off == 0:
                out[0, :, h * width : (h + 1) * width] = binned
                continue
            c_out[off - 1, h] = binned.astype(jnp.bfloat16)
            copy = pltpu.make_async_remote_copy(
                src_ref=c_out.at[off - 1, h],
                dst_ref=c_in.at[off - 1, h],
                send_sem=c_send.at[off - 1, h],
                recv_sem=c_recv.at[off - 1, h],
                device_id=(chan_peer[off], tm),
                device_id_type=MESH,
            )
            copy.start()
            c_copies[h].append(copy)
    for h in range(CHUNKS):
        total = out[0, :, h * width : (h + 1) * width]
        for n, copy in enumerate(c_copies[h]):
            copy.wait_recv()
            total = total + c_in[n, h].astype(jnp.float32)
        out[0, :, h * width : (h + 1) * width] = total
    for copy in slab_copies + sum(t_copies, []) + sum(c_copies, []):
        copy.wait_send()


def per_device(n_chan, n_tm, spectra, tile_bin, owner_bins, source_slab):
    _, channels, columns = spectra.shape
    rows = channels // n_tm
    width = LAGS // CHUNKS
    smem = pl.BlockSpec(memory_space=pltpu.SMEM)
    anywhere = pl.BlockSpec(memory_space=pl.ANY)
    dma = pltpu.SemaphoreType.DMA
    return pl.pallas_call(
        functools.partial(kernel, n_chan, n_tm),
        out_shape=jax.ShapeDtypeStruct((1, rows, LAGS), jnp.float32),
        in_specs=[smem, smem, smem, anywhere, anywhere],
        out_specs=pl.BlockSpec(memory_space=pltpu.VMEM),
        scratch_shapes=[
            pltpu.VMEM((channels, columns), jnp.bfloat16),
            pltpu.VMEM((columns, LAGS), jnp.bfloat16),
            pltpu.VMEM((channels, columns), jnp.float32),
            pltpu.VMEM((n_chan, SRC * columns // WIDE, WIDE), jnp.bfloat16),
            pltpu.VMEM((SRC * rows, LAGS), jnp.float32),
            pltpu.VMEM((n_tm - 1, CHUNKS, SRC * rows, width), jnp.bfloat16),
            pltpu.VMEM((n_tm - 1, CHUNKS, SRC * rows, width), jnp.bfloat16),
            pltpu.VMEM((n_chan - 1, CHUNKS, rows, width), jnp.bfloat16),
            pltpu.VMEM((n_chan - 1, CHUNKS, rows, width), jnp.bfloat16),
            dma((2,)),
            dma((n_chan - 1,)),
            dma((n_chan - 1,)),
            dma((n_tm - 1, CHUNKS)),
            dma((n_tm - 1, CHUNKS)),
            dma((n_chan - 1, CHUNKS)),
            dma((n_chan - 1, CHUNKS)),
        ],
        compiler_params=pltpu.CompilerParams(
            collective_id=0, has_side_effects=True, vmem_limit_bytes=32 * 1024 * 1024
        ),
        name="stack_kernel",
    )(tile_bin, owner_bins, source_slab, spectra, phase_table(columns // 2))


def solution(mesh):
    return jax.shard_map(
        functools.partial(per_device, mesh.shape["chan"], mesh.shape["tm"]),
        mesh=mesh,
        in_specs=(P("tm", "chan", None), P("chan"), P(), P()),
        out_specs=P("chan", "tm", None),
        check_vma=False,
    )
```

time: 136 us -> 27.7 us (0.20)
  waiting for transfers between devices: 100 us -> 0 us
  Pallas kernels: 0 us -> 24 us
  between operations: 14.2 us -> 0.71 us
  other arithmetic: 8.38 us -> 0 us
  starting transfers between devices: 6.27 us -> 0 us
  matrix products: 1.77 us -> 0 us
  local copies, waits for them, and re-layouts: 4.45 us -> 2.81 us
    psum x1 -> x0, waiting for transfers between devices: 50.9 us -> none  [per_device(): summed = lax.psum(traces, 'tm')]
    reduce_scatter x1 -> x0, waiting for transfers between devices: 31.1 us -> none  [per_device(): lax.psum_scatter(jnp.einsum('rt,tpl->rpl', membership, own_rows, precisio...]
    pallas_call x0 -> x1, Pallas kernels: none -> 24 us  [per_device(): pl.pallas_call(functools.partial(kernel, n_chan, n_tm), out_shape=jax.Sha...]
    ppermute x8 -> x0, waiting for transfers between devices: 18.1 us -> none  [shifted(): return lax.ppermute(block, axis, route)]
    ppermute x8 -> x0, starting transfers between devices: 6.23 us -> none  [shifted(): return lax.ppermute(block, axis, route)]
    cos x1 -> x0, other arithmetic: 4.29 us -> none  [phase_tables(): return (jnp.cos(angle), jnp.sin(angle))]
    div x2 -> x0, other arithmetic: 2.58 us -> none  [the longest x1 1.47 us: per_device(): return stacked / lax.axis_size('tm')]
    dynamic_slice x2 -> x0, local copies, waits for them, and re-layouts: 1.89 us -> none  [per_device(): lax.dynamic_slice_in_dim(summed, lax.axis_index('tm') * row_count, row_co...]
  transfers between devices with their start and end apart: 10 -> 0, of which waited for: 10 -> 0; matrix products, arithmetic and copies ran while one was open for 0% -> 0% of each run, Pallas kernels for 0% -> 0%
where the time goes in v1:
time: 27.7 us; the launch traced here: 27.6 us
  Pallas kernels  24 us (87%)
  local copies, waits for them, and re-layouts  2.81 us (10%)
  between operations  0.71 us (3%)
    pallas_call x1, Pallas kernels, per_device(): pl.pallas_call(functools.partial(kernel, n_chan, n_tm), out_shape=jax.Sha...  24 us
    unnamed x9, local copies, waits for them, and re-layouts  2.81 us

profile of v1, /device:TPU:0, one launch (start us, length us, event | category | flops | bytes accessed | tf_op | source)
XLA Modules:
  0.0 27.6 jit_solution(7974569567875139830)
XLA Ops:
  0.0 0.0 copy-start.3
  0.0 0.0 copy-start.2
  0.7 0.0 copy-done.3
  0.7 0.0 copy-done.2
  0.7 0.0 copy-start
  0.7 1.2 %copy-done = bf16[1024,512]{1,0:T(8,128)(2,1)S(1)} copy-done((bf16[1024,512]{1,0:T(8,128)(2,1)S(1)}, bf16[1024,512]{1,0:T(8,128)(2,1)}, u32[]{:S(2)}) %copy-start) | copy-done | bytes 1048600
  1.9 0.0 copy-start.1
  1.9 0.9 %copy-done.1 = bf16[1,128,1024]{2,1,0:T(8,128)(2,1)S(1)} copy-done((bf16[1,128,1024]{2,1,0:T(8,128)(2,1)S(1)}, bf16[1,128,1024]{2,1,0:T(8,128)(2,1)}, u32[]{:S(2)}) %copy-start.1) | copy-done | bytes 262168
  2.9 24.0 %stack_kernel.1 = f32[1,32,512]{2,1,0:T(8,128)S(1)} custom-call(s32[4]{0:T(128)S(1)} %copy-done.2, s32[8]{0:T(128)S(1)} %copy-done.3, s32[1]{0:T(128)S(6)} %copy.7.source_slab, bf16[1,128,1024]{2,1,0:T(8,128)(2,1)S(1)} %copy-done.1, bf16[1024,512]{1,0:T(8,128)(2,1)S(1)} %copy-done), custom_call_target="tpu_custom_call" | custom-call | tf_op jit(solution)/shard_map/stack_kernel/pallas_call | solution.py:206
  26.9 0.6 %copy.8 = f32[1,32,512]{2,1,0:T(8,128)} copy(f32[1,32,512]{2,1,0:T(8,128)S(1)} %stack_kernel.1) | data formatting | bytes 131072
Async XLA Ops:
  0.0 0.7 %copy-start.3 = (s32[8]{0:T(128)S(1)}, s32[8]{0:T(128)}, u32[]{:S(2)}) copy-start(s32[8]{0:T(128)} %owner_bins.1) | copy-start | bytes 100
  0.0 0.7 %copy-start.2 = (s32[4]{0:T(128)S(1)}, s32[4]{0:T(128)}, u32[]{:S(2)}) copy-start(s32[4]{0:T(128)} %tile_bin.1) | copy-start | bytes 52
  0.7 1.2 %copy-start = (bf16[1024,512]{1,0:T(8,128)(2,1)S(1)}, bf16[1024,512]{1,0:T(8,128)(2,1)}, u32[]{:S(2)}) copy-start(bf16[1024,512]{1,0:T(8,128)(2,1)} %constant.2.clone.table_in) | copy-start | bytes 3145732
  1.9 0.9 %copy-start.1 = (bf16[1,128,1024]{2,1,0:T(8,128)(2,1)S(1)}, bf16[1,128,1024]{2,1,0:T(8,128)(2,1)}, u32[]{:S(2)}) copy-start(bf16[1,128,1024]{2,1,0:T(8,128)(2,1)} %spectra.1) | copy-start | bytes 786436

commit v2 on v1

--- a/solution.py
+++ b/solution.py
@@ -40,8 +40,8 @@
 
 
 def kernel(
-    n_chan, n_tm, tile_bin, owner_bins, source_slab, spectra, table_in, out,
-    block, table, white, slabs, own, t_out, t_in, c_out, c_in,
+    n_chan, n_tm, tile_in, owner_in, slab_in, spectra, table_in, out,
+    tile_bin, owner_bins, source_slab, block, table, white, slabs, own, t_out, t_in, c_out, c_in,
     local_sems, s_send, s_recv, t_send, t_recv, c_send, c_recv,
 ):
     channels, columns = block.shape
@@ -69,9 +69,13 @@
         pl.semaphore_signal(barrier, inc=1, device_id=(chan, tm_peer[off]), device_id_type=MESH)
     load_block = pltpu.make_async_copy(spectra.at[0], block, local_sems.at[0])
     load_table = pltpu.make_async_copy(table_in, table, local_sems.at[1])
-    load_block.start()
-    load_table.start()
-
+    load_slab = pltpu.make_async_copy(slab_in, source_slab, local_sems.at[2])
+    load_tiles = pltpu.make_async_copy(tile_in, tile_bin, local_sems.at[3])
+    load_owners = pltpu.make_async_copy(owner_in, owner_bins, local_sems.at[4])
+    for load in (load_slab, load_block, load_tiles, load_owners, load_table):
+        load.start()
+
+    load_slab.wait()
     slab = source_slab[0]
     slabs_per_block = channels // SRC
     root = slab // slabs_per_block
@@ -124,7 +128,8 @@
     source_real, source_imag = whiten(
         source[: SRC * halves], source[SRC * halves :], same_group
     )
-    load_table.wait()
+    for load in (load_tiles, load_owners, load_table):
+        load.wait()
 
     t_copies = [[] for _ in range(CHUNKS)]
     for off in [*reversed(range(1, n_tm)), 0]:
@@ -157,8 +162,10 @@
                 device_id=(chan, tm_peer[off]),
                 device_id_type=MESH,
             )
-            copy.start()
             t_copies[h].append(copy)
+
+    for copy in sum(t_copies, []):
+        copy.start()
 
     c_copies = [[] for _ in range(CHUNKS)]
     for h in range(CHUNKS):
@@ -200,15 +207,17 @@
     _, channels, columns = spectra.shape
     rows = channels // n_tm
     width = LAGS // CHUNKS
-    smem = pl.BlockSpec(memory_space=pltpu.SMEM)
-    anywhere = pl.BlockSpec(memory_space=pl.ANY)
+    in_place = pl.BlockSpec(memory_space=pltpu.HBM)
     dma = pltpu.SemaphoreType.DMA
     return pl.pallas_call(
         functools.partial(kernel, n_chan, n_tm),
         out_shape=jax.ShapeDtypeStruct((1, rows, LAGS), jnp.float32),
-        in_specs=[smem, smem, smem, anywhere, anywhere],
+        in_specs=[in_place] * 5,
         out_specs=pl.BlockSpec(memory_space=pltpu.VMEM),
         scratch_shapes=[
+            pltpu.SMEM(tile_bin.shape, jnp.int32),
+            pltpu.SMEM(owner_bins.shape, jnp.int32),
+            pltpu.SMEM(source_slab.shape, jnp.int32),
             pltpu.VMEM((channels, columns), jnp.bfloat16),
             pltpu.VMEM((columns, LAGS), jnp.bfloat16),
             pltpu.VMEM((channels, columns), jnp.float32),
@@ -218,7 +227,7 @@
             pltpu.VMEM((n_tm - 1, CHUNKS, SRC * rows, width), jnp.bfloat16),
             pltpu.VMEM((n_chan - 1, CHUNKS, rows, width), jnp.bfloat16),
             pltpu.VMEM((n_chan - 1, CHUNKS, rows, width), jnp.bfloat16),
-            dma((2,)),
+            dma((5,)),
             dma((n_chan - 1,)),
             dma((n_chan - 1,)),
             dma((n_tm - 1, CHUNKS)),
@@ -227,7 +236,7 @@
             dma((n_chan - 1, CHUNKS)),
         ],
         compiler_params=pltpu.CompilerParams(
-            collective_id=0, has_side_effects=True, vmem_limit_bytes=32 * 1024 * 1024
+            collective_id=0, has_side_effects=True, vmem_limit_bytes=55040 * 1024
         ),
         name="stack_kernel",
     )(tile_bin, owner_bins, source_slab, spectra, phase_table(columns // 2))

time: 27.7 us -> 23.9 us (0.86)
  local copies, waits for them, and re-layouts: 2.81 us -> 0.64 us
  Pallas kernels: 24 us -> 22.3 us
    unnamed x9 -> x5, local copies, waits for them, and re-layouts: 2.81 us -> 0.64 us
    pallas_call x1, Pallas kernels: 24 us -> 22.3 us  [per_device(): pl.pallas_call(functools.partial(kernel, n_chan, n_tm), out_shape=jax.Sha...]
where the time goes in v2:
time: 23.9 us; the launch traced here: 23.7 us
  Pallas kernels  22.3 us (93%)
  between operations  0.7 us (3%)
  local copies, waits for them, and re-layouts  0.64 us (3%)
    pallas_call x1, Pallas kernels, per_device(): pl.pallas_call(functools.partial(kernel, n_chan, n_tm), out_shape=jax.Sha...  22.3 us
    unnamed x5, local copies, waits for them, and re-layouts  0.64 us

profile of v2, /device:TPU:0, one launch (start us, length us, event | category | flops | bytes accessed | tf_op | source)
XLA Modules:
  0.0 23.7 jit_solution(2134559543861894119)
XLA Ops:
  0.0 0.0 copy-start.1
  0.0 0.0 copy-start
  0.7 0.0 copy-done.1
  0.7 0.0 copy-done
  0.7 22.3 %stack_kernel.1 = f32[1,32,512]{2,1,0:T(8,128)S(1)} custom-call(s32[4]{0:T(128)S(1)} %copy-done, s32[8]{0:T(128)S(1)} %copy-done.1, s32[1]{0:T(128)S(6)} %copy.7.slab_in, bf16[1,128,1024]{2,1,0:T(8,128)(2,1)} %spectra.1, bf16[1024,512]{1,0:T(8,128)(2,1)} %constant.2.clone.table_in), custom_call_target="tpu_custom_call" | custom-call | tf_op jit(solution)/shard_map/stack_kernel/pallas_call | solution.py:212
  23.0 0.6 %copy.8 = f32[1,32,512]{2,1,0:T(8,128)} copy(f32[1,32,512]{2,1,0:T(8,128)S(1)} %stack_kernel.1) | data formatting | bytes 131072
Async XLA Ops:
  0.0 0.7 %copy-start.1 = (s32[8]{0:T(128)S(1)}, s32[8]{0:T(128)}, u32[]{:S(2)}) copy-start(s32[8]{0:T(128)} %owner_in.1) | copy-start | bytes 100
  0.0 0.7 %copy-start = (s32[4]{0:T(128)S(1)}, s32[4]{0:T(128)}, u32[]{:S(2)}) copy-start(s32[4]{0:T(128)} %tile_in.1) | copy-start | bytes 52

commit v3 on v2

--- a/solution.py
+++ b/solution.py
@@ -16,14 +16,25 @@
 SRC = 4
 PAIRS = 128
 WIDE = 256
-CHUNKS = 2
+RANK = 128
 MESH = pl.DeviceIdType.MESH
 
 
-def phase_table(bands):
-    phase = (K0 + np.arange(bands))[:, None] * (np.arange(LAGS) - LAGS // 2)[None, :] % SEG_LEN
+def phase_factors(bands):
+    lag_index = np.arange(LAGS) - LAGS // 2
+    phase = (K0 + np.arange(bands))[:, None] * lag_index[None, :] % SEG_LEN
     angle = phase.astype(np.float64) * (2.0 * math.pi / SEG_LEN)
-    return jnp.asarray(np.concatenate([np.cos(angle), np.sin(angle)]), dtype=jnp.bfloat16)
+    waves = np.concatenate([np.cos(angle), np.sin(angle)])
+    grid = (lag_index + 0.5) / (LAGS / 2)
+    basis = np.full((1, LAGS), LAGS**-0.5)
+    while len(basis) < RANK:
+        row = grid * basis[-1]
+        for _ in range(2):
+            row = row - np.sum(np.sum(basis * row, axis=1, keepdims=True) * basis, axis=0)
+        basis = np.concatenate([basis, row[None] / np.sqrt(np.sum(row * row))])
+    factor = waves @ basis.T
+    assert np.abs(factor @ basis - waves).max() < 1e-9
+    return jnp.asarray(factor, jnp.bfloat16), jnp.asarray(basis, jnp.float32)
 
 
 def whiten(real_part, imag_part, same_group):
@@ -40,15 +51,14 @@
 
 
 def kernel(
-    n_chan, n_tm, tile_in, owner_in, slab_in, spectra, table_in, out,
-    tile_bin, owner_bins, source_slab, block, table, white, slabs, own, t_out, t_in, c_out, c_in,
+    n_chan, n_tm, tile_in, owner_in, slab_in, spectra, table_in, basis_in, out,
+    tile_bin, owner_bins, source_slab, block, table, basis, white, slabs, own, t_out, t_in, c_out, c_in,
     local_sems, s_send, s_recv, t_send, t_recv, c_send, c_recv,
 ):
     channels, columns = block.shape
     bands = columns // 2
     halves = bands // WIDE
     rows = channels // n_tm
-    width = LAGS // CHUNKS
     chan = lax.axis_index("chan")
     tm = lax.axis_index("tm")
     near = 1
@@ -72,7 +82,8 @@
     load_slab = pltpu.make_async_copy(slab_in, source_slab, local_sems.at[2])
     load_tiles = pltpu.make_async_copy(tile_in, tile_bin, local_sems.at[3])
     load_owners = pltpu.make_async_copy(owner_in, owner_bins, local_sems.at[4])
-    for load in (load_slab, load_block, load_tiles, load_owners, load_table):
+    load_basis = pltpu.make_async_copy(basis_in, basis, local_sems.at[5])
+    for load in (load_slab, load_block, load_tiles, load_owners, load_table, load_basis):
         load.start()
 
     load_slab.wait()
@@ -131,7 +142,7 @@
     for load in (load_tiles, load_owners, load_table):
         load.wait()
 
-    t_copies = [[] for _ in range(CHUNKS)]
+    t_copies = []
     for off in [*reversed(range(1, n_tm)), 0]:
         at = pl.ds(pl.multiple_of(tm_peer[off] * rows, rows), rows)
         products = []
@@ -147,99 +158,98 @@
             products.append(jnp.concatenate(upper + lower, axis=1))
         product = jnp.concatenate(products, axis=0).astype(jnp.bfloat16)
         correlation = jnp.dot(product, table[...], preferred_element_type=jnp.float32)
-        energy = jnp.mean(correlation * correlation, axis=-1, keepdims=True)
+        energy = jnp.sum(correlation * correlation, axis=-1, keepdims=True) * (1.0 / LAGS)
         traces = correlation * (lax.rsqrt(energy + 1e-06) * (1.0 / n_tm))
         if off == 0:
             own[...] = traces
             continue
-        for h in range(CHUNKS):
-            t_out[off - 1, h] = traces[:, h * width : (h + 1) * width].astype(jnp.bfloat16)
-            copy = pltpu.make_async_remote_copy(
-                src_ref=t_out.at[off - 1, h],
-                dst_ref=t_in.at[off - 1, h],
-                send_sem=t_send.at[off - 1, h],
-                recv_sem=t_recv.at[off - 1, h],
-                device_id=(chan, tm_peer[off]),
-                device_id_type=MESH,
-            )
-            t_copies[h].append(copy)
-
-    for copy in sum(t_copies, []):
+        t_out[off - 1] = traces.astype(jnp.bfloat16)
+        copy = pltpu.make_async_remote_copy(
+            src_ref=t_out.at[off - 1],
+            dst_ref=t_in.at[off - 1],
+            send_sem=t_send.at[off - 1],
+            recv_sem=t_recv.at[off - 1],
+            device_id=(chan, tm_peer[off]),
+            device_id_type=MESH,
+        )
         copy.start()
-
-    c_copies = [[] for _ in range(CHUNKS)]
-    for h in range(CHUNKS):
-        summed = own[:, h * width : (h + 1) * width]
-        for n, copy in enumerate(t_copies[h]):
-            copy.wait_recv()
-            summed = summed + t_in[n_tm - 2 - n, h].astype(jnp.float32)
-        for off in [*range(1, n_chan), 0]:
-            bin_here = owner_bins[chan_peer[off]]
-            binned = jnp.zeros((rows, width), jnp.float32)
-            for i in range(SRC):
-                member = jnp.where(tile_bin[i] == bin_here, 1.0, 0.0)
-                binned = binned + summed[i * rows : (i + 1) * rows] * member
-            if off == 0:
-                out[0, :, h * width : (h + 1) * width] = binned
-                continue
-            c_out[off - 1, h] = binned.astype(jnp.bfloat16)
-            copy = pltpu.make_async_remote_copy(
-                src_ref=c_out.at[off - 1, h],
-                dst_ref=c_in.at[off - 1, h],
-                send_sem=c_send.at[off - 1, h],
-                recv_sem=c_recv.at[off - 1, h],
-                device_id=(chan_peer[off], tm),
-                device_id_type=MESH,
-            )
-            copy.start()
-            c_copies[h].append(copy)
-    for h in range(CHUNKS):
-        total = out[0, :, h * width : (h + 1) * width]
-        for n, copy in enumerate(c_copies[h]):
-            copy.wait_recv()
-            total = total + c_in[n, h].astype(jnp.float32)
-        out[0, :, h * width : (h + 1) * width] = total
-    for copy in slab_copies + sum(t_copies, []) + sum(c_copies, []):
+        t_copies.append(copy)
+
+    members = [
+        [jnp.where(tile_bin[i] == owner_bins[peer], 1.0, 0.0) for i in range(SRC)]
+        for peer in chan_peer
+    ]
+    summed = own[...]
+    for n, copy in reversed([*enumerate(t_copies)]):
+        copy.wait_recv()
+        summed = summed + t_in[n_tm - 2 - n].astype(jnp.float32)
+    c_copies = []
+    for off in [*range(1, n_chan), 0]:
+        binned = jnp.zeros((rows, RANK), jnp.float32)
+        for i in range(SRC):
+            binned = binned + summed[i * rows : (i + 1) * rows] * members[off][i]
+        if off == 0:
+            total = binned
+            continue
+        c_out[off - 1] = binned.astype(jnp.bfloat16)
+        copy = pltpu.make_async_remote_copy(
+            src_ref=c_out.at[off - 1],
+            dst_ref=c_in.at[off - 1],
+            send_sem=c_send.at[off - 1],
+            recv_sem=c_recv.at[off - 1],
+            device_id=(chan_peer[off], tm),
+            device_id_type=MESH,
+        )
+        copy.start()
+        c_copies.append(copy)
+    load_basis.wait()
+    for n, copy in enumerate(c_copies):
+        copy.wait_recv()
+        total = total + c_in[n].astype(jnp.float32)
+    out[0] = jnp.dot(
+        total, basis[...], precision=lax.Precision.HIGHEST, preferred_element_type=jnp.float32
+    )
+    for copy in slab_copies + t_copies + c_copies:
         copy.wait_send()
 
 
 def per_device(n_chan, n_tm, spectra, tile_bin, owner_bins, source_slab):
     _, channels, columns = spectra.shape
     rows = channels // n_tm
-    width = LAGS // CHUNKS
     in_place = pl.BlockSpec(memory_space=pltpu.HBM)
     dma = pltpu.SemaphoreType.DMA
     return pl.pallas_call(
         functools.partial(kernel, n_chan, n_tm),
         out_shape=jax.ShapeDtypeStruct((1, rows, LAGS), jnp.float32),
-        in_specs=[in_place] * 5,
+        in_specs=[in_place] * 6,
         out_specs=pl.BlockSpec(memory_space=pltpu.VMEM),
         scratch_shapes=[
             pltpu.SMEM(tile_bin.shape, jnp.int32),
             pltpu.SMEM(owner_bins.shape, jnp.int32),
             pltpu.SMEM(source_slab.shape, jnp.int32),
             pltpu.VMEM((channels, columns), jnp.bfloat16),
-            pltpu.VMEM((columns, LAGS), jnp.bfloat16),
+            pltpu.VMEM((columns, RANK), jnp.bfloat16),
+            pltpu.VMEM((RANK, LAGS), jnp.float32),
             pltpu.VMEM((channels, columns), jnp.float32),
             pltpu.VMEM((n_chan, SRC * columns // WIDE, WIDE), jnp.bfloat16),
-            pltpu.VMEM((SRC * rows, LAGS), jnp.float32),
-            pltpu.VMEM((n_tm - 1, CHUNKS, SRC * rows, width), jnp.bfloat16),
-            pltpu.VMEM((n_tm - 1, CHUNKS, SRC * rows, width), jnp.bfloat16),
-            pltpu.VMEM((n_chan - 1, CHUNKS, rows, width), jnp.bfloat16),
-            pltpu.VMEM((n_chan - 1, CHUNKS, rows, width), jnp.bfloat16),
-            dma((5,)),
-            dma((n_chan - 1,)),
-            dma((n_chan - 1,)),
-            dma((n_tm - 1, CHUNKS)),
-            dma((n_tm - 1, CHUNKS)),
-            dma((n_chan - 1, CHUNKS)),
-            dma((n_chan - 1, CHUNKS)),
+            pltpu.VMEM((SRC * rows, RANK), jnp.float32),
+            pltpu.VMEM((n_tm - 1, SRC * rows, RANK), jnp.bfloat16),
+            pltpu.VMEM((n_tm - 1, SRC * rows, RANK), jnp.bfloat16),
+            pltpu.VMEM((n_chan - 1, rows, RANK), jnp.bfloat16),
+            pltpu.VMEM((n_chan - 1, rows, RANK), jnp.bfloat16),
+            dma((6,)),
+            dma((n_chan - 1,)),
+            dma((n_chan - 1,)),
+            dma((n_tm - 1,)),
+            dma((n_tm - 1,)),
+            dma((n_chan - 1,)),
+            dma((n_chan - 1,)),
         ],
         compiler_params=pltpu.CompilerParams(
             collective_id=0, has_side_effects=True, vmem_limit_bytes=55040 * 1024
         ),
         name="stack_kernel",
-    )(tile_bin, owner_bins, source_slab, spectra, phase_table(columns // 2))
+    )(tile_bin, owner_bins, source_slab, spectra, *phase_factors(columns // 2))
 
 
 def solution(mesh):

time: 23.9 us -> 19.9 us (0.83)
  Pallas kernels: 22.3 us -> 18.4 us
    pallas_call x1, Pallas kernels: 22.3 us -> 18.4 us  [per_device(): pl.pallas_call(functools.partial(kernel, n_chan, n_tm), out_shape=jax.Sha...]
where the time goes in v3:
time: 19.9 us; the launch traced here: 19.8 us
  Pallas kernels  18.4 us (92%)
  between operations  0.7 us (4%)
  local copies, waits for them, and re-layouts  0.64 us (3%)
    pallas_call x1, Pallas kernels, per_device(): pl.pallas_call(functools.partial(kernel, n_chan, n_tm), out_shape=jax.Sha...  18.4 us
    unnamed x5, local copies, waits for them, and re-layouts  0.64 us

profile of v3, /device:TPU:0, one launch (start us, length us, event | category | flops | bytes accessed | tf_op | source)
XLA Modules:
  0.0 19.8 jit_solution(906683752639680202)
XLA Ops:
  0.0 0.0 copy-start.1
  0.0 0.0 copy-start
  0.7 0.0 copy-done.1
  0.7 0.0 copy-done
  0.7 18.4 %stack_kernel.1 = f32[1,32,512]{2,1,0:T(8,128)S(1)} custom-call(s32[4]{0:T(128)S(1)} %copy-done, s32[8]{0:T(128)S(1)} %copy-done.1, s32[1]{0:T(128)S(6)} %copy.8.slab_in, bf16[1,128,1024]{2,1,0:T(8,128)(2,1)} %spectra.1, bf16[1024,128]{1,0:T(8,128)(2,1)} %constant.4.clone.table_in, f32[128,512]{1,0:T(8,128)} %constant.5.clone.basis_in), custom_call_target="tpu_custom_call" | custom-call | tf_op jit(solution)/shard_map/stack_kernel/pallas_call | solution.py:221
  19.1 0.6 %copy.9 = f32[1,32,512]{2,1,0:T(8,128)} copy(f32[1,32,512]{2,1,0:T(8,128)S(1)} %stack_kernel.1) | data formatting | bytes 131072
Async XLA Ops:
  0.0 0.7 %copy-start.1 = (s32[8]{0:T(128)S(1)}, s32[8]{0:T(128)}, u32[]{:S(2)}) copy-start(s32[8]{0:T(128)} %owner_in.1) | copy-start | bytes 100
  0.0 0.7 %copy-start = (s32[4]{0:T(128)S(1)}, s32[4]{0:T(128)}, u32[]{:S(2)}) copy-start(s32[4]{0:T(128)} %tile_in.1) | copy-start | bytes 52
